TPU v7x, 32 devices: a whole 2x2x4 slice. The times are simulated.
32 devices in a mesh: grp: 2 (over y), col: 4 (over z), row: 2 (over x), seq: 2 (over core).
Axes of the slice: x: 2, y: 2, z: 4, core: 2. Of those that a mesh axis runs over, the one named last changes fastest.
Arguments:
- alignment_tensor: float32 [192, 2, 128, 64], P(('grp', 'seq'), 'row', 'col'), parts along dimension 0, may hold values from -6 to 6
- residue_couplings: float32 [512, 256, 128], P(('grp', 'row'), 'col'), parts along dimension 0, may hold values from -6 to 6
- first_factor_matrix: float32 [64, 32], replicated, may hold values from -0.75 to 0.75
- second_factor_matrix: float32 [64, 32], replicated, may hold values from -0.75 to 0.75
- tensor_product_matrix: float32 [1024, 128], replicated, may hold values from -0.1875 to 0.1875
- coupling_score_matrix: float32 [128, 8], replicated, may hold values from -10.606602 to 10.606602
- averaged_source_matrix: float32 [64, 256], replicated, may hold values from -0.75 to 0.75
- sigmoid_matrix: float32 [64, 256], replicated, may hold values from -0.75 to 0.75
- final_matrix: float32 [256, 64], replicated, may hold values from -0.375 to 0.375
Outputs:
- revised_alignment: float32 [192, 2, 128, 64], P(('grp', 'seq'), 'row', 'col'), parts along dimension 0
- revised_couplings: float32 [512, 256, 128], P(('grp', 'row'), 'col'), parts along dimension 0
There are 2 independent parts, one for each index of `grp`. A program takes and returns all parts, laid end to end along the dimension named above; an argument that names none is the same for every part. Nothing has to cross between parts.
All inputs are finite; a program needn't handle non-finite values.
Results may differ from a plain program's by a relative error of at most 0.0003.
Values sent between devices are 32-bit elements; how exact they have to be, the bound alone decides.
A program may use at most 64 MiB of HBM per device.

v0:
```python
import jax
import jax.numpy as jnp
from jax import lax
from jax.sharding import PartitionSpec as P

epsilon = 1e-05
exact_arithmetic = lax.Precision.HIGHEST


def broadcast(block, axis, holder):
    block = jnp.where(lax.axis_index(axis) == holder, block, jnp.zeros_like(block))
    return lax.psum(block, axis)


def standardize_entries(inputs):
    center = inputs - jnp.mean(inputs, axis=-1, keepdims=True)
    spread = jnp.mean(center * center, axis=-1, keepdims=True)
    return center / jnp.sqrt(spread + epsilon)


def pair_scores(pair_rows, coupling_score_matrix):
    return jnp.einsum(
        "ijc,ch->ihj",
        standardize_entries(pair_rows),
        coupling_score_matrix,
        precision=exact_arithmetic,
    )


def on_device(
    alignment_tensor,
    residue_couplings,
    first_factor_matrix,
    second_factor_matrix,
    tensor_product_matrix,
    coupling_score_matrix,
    averaged_source_matrix,
    sigmoid_matrix,
    final_matrix,
):
    shard_alignment_entries = alignment_tensor.shape[0]
    total_seqs = shard_alignment_entries * lax.axis_size("seq")
    coupling_lines = residue_couplings.shape[0]
    col_count = residue_couplings.shape[1]
    alignment_depth = alignment_tensor.shape[3]
    outer_width = first_factor_matrix.shape[1]
    head_count = coupling_score_matrix.shape[1]
    gathered_lines = lax.all_gather(alignment_tensor, "col", axis=2, tiled=True)
    alignment_tile_entries = gathered_lines.reshape(
        shard_alignment_entries, coupling_lines, alignment_depth
    )
    standardized_alignment = standardize_entries(alignment_tile_entries)
    first_factor_tile = jnp.einsum(
        "kgd,dl->kgl", standardized_alignment, first_factor_matrix, precision=exact_arithmetic
    )
    combined_matrix = jnp.concatenate([second_factor_matrix, averaged_source_matrix], axis=1)
    first_col = lax.axis_index("col") * col_count
    root_row = first_col // coupling_lines
    offset = first_col % coupling_lines
    raw_piece = lax.dynamic_slice_in_dim(alignment_tile_entries, offset, col_count, 1)
    raw_received = broadcast(raw_piece, "row", root_row)
    received = jnp.einsum(
        "pko,ol->pkl",
        standardize_entries(raw_received),
        combined_matrix,
        precision=exact_arithmetic,
    )
    second_factor_tile = received[:, :, :outer_width]
    averaged_sources = received[:, :, outer_width:].reshape(
        shard_alignment_entries, col_count, head_count, -1
    )
    block_rows = 16
    left_blocks = first_factor_tile.reshape(
        shard_alignment_entries, coupling_lines // block_rows, block_rows, outer_width
    ).transpose(1, 0, 2, 3)

    def outer_block(left_block):
        product = (
            jnp.einsum("sic,sje->ijce", left_block, second_factor_tile, precision=exact_arithmetic)
            / total_seqs
        )
        flat_prod = product.reshape(block_rows * col_count, -1)
        return jnp.dot(flat_prod, tensor_product_matrix, precision=exact_arithmetic).reshape(
            block_rows, col_count, -1
        )

    update = lax.map(outer_block, left_blocks).reshape(coupling_lines, col_count, -1)
    revised_couplings = residue_couplings + lax.psum(update, "seq")
    scores = pair_scores(revised_couplings, coupling_score_matrix)
    local_top = jnp.max(scores, axis=2)
    score_top = lax.pmax(local_top, "col")
    score_total = lax.psum(jnp.sum(jnp.exp(scores - score_top[:, :, None]), axis=2), "col")
    weights = jnp.exp(scores - score_top[:, :, None]) / score_total[:, :, None]
    mixed_rows = jnp.einsum(
        "ihj,sjhd->sihd", weights, averaged_sources, precision=exact_arithmetic
    ).reshape(shard_alignment_entries, coupling_lines, -1)
    summed = lax.psum_scatter(mixed_rows, "col", scatter_dimension=1, tiled=True)
    shard_standardized_alignment = standardize_entries(
        alignment_tensor.reshape(shard_alignment_entries, -1, alignment_depth)
    )
    sigmoid_factors = jax.nn.sigmoid(
        jnp.einsum(
            "pko,ol->pkl", shard_standardized_alignment, sigmoid_matrix, precision=exact_arithmetic
        )
    )
    coupling_increment = jnp.einsum(
        "snf,fc->snc", summed * sigmoid_factors, final_matrix, precision=exact_arithmetic
    )
    revised_alignment = alignment_tensor + coupling_increment.reshape(alignment_tensor.shape)
    return (revised_alignment, revised_couplings)


def solution(mesh):
    return jax.shard_map(
        on_device,
        mesh=mesh,
        in_specs=(
            P(("grp", "seq"), "row", "col", None),
            P(("grp", "row"), "col", None),
            P(),
            P(),
            P(),
            P(),
            P(),
            P(),
            P(),
        ),
        out_specs=(P(("grp", "seq"), "row", "col", None), P(("grp", "row"), "col", None)),
        check_vma=False,
    )
```

profile of v0, /device:TPU:0, one launch (start us, length us, event | category | flops | bytes accessed | tf_op | source)
XLA Modules:
  0.0 611.7 jit_solution(10062360906110681422)
XLA Ops:
  7.2 0.7 all-gather.2.cloned.1.call-update
  7.9 0.0 all-reduce.3.cloned.1.call-start
  8.0 0.8 copy.37
  8.8 67.0 %all-gather.2.cloned.1.call-done = f32[48,1,128,64]{3,2,1,0:T(8,128)} async-done(((f32[48,1,32,64]{3,2,1,0:T(8,128)}), f32[48,1,128,64]{3,2,1,0:T(8,128)}) %all-gather.2.cloned.1.call-update) | async-done | bytes 1572880 | tf_op jit(solution)/shard_map/all_gather | solution.py:48
  75.8 2.9 select_bitcast_fusion
  78.7 0.0 all-reduce.5.cloned.1.call-start
  78.8 0.9 reduce_sum.83
  79.7 1.8 fusion.12
  81.5 0.1 copy.39
  81.6 0.1 copy.41
  81.7 12.2 %fusion.21 = f32[8,48,16,32]{1,3,2,0:T(8,128)} fusion(f32[48,8,16,64]{3,2,1,0:T(8,128)S(1)} %bitcast.95, f32[48,8,16]{0,2,1:T(8,128)S(1)} %bitcast.98, f32[48,8,16]{0,2,1:T(8,128)S(1)} %bitcast.97, f32[64,32]{0,1:T(8,128)S(1)} %copy-done.9), kind=kOutput, calls=%fused_computation.23 | convolution fusion | flops 151781376 | bytes 2416640 | tf_op jit(solution)/shard_map/kgd,dl->kgl/dot_general | solution.py:53
  93.9 35.1 %all-reduce.3.cloned.1.call-done = f32[48,64,64]{2,1,0:T(8,128)} async-done(((f32[48,64,64]{2,1,0:T(8,128)}), f32[48,64,64]{2,1,0:T(8,128)}) %all-reduce.3.cloned.1.call-update) | async-done | bytes 786448 | tf_op jit(solution)/shard_map/psum | solution.py:12
  129.0 2.0 reduce_sum.81
  131.1 2.3 multiply_reduce_fusion.1
  133.4 4.7 fusion.31
  138.1 2.1 copy-done.2
  140.2 0.1 slice.9
  140.3 0.5 copy.42
  140.9 0.4 copy-done.5
  141.3 245.4 %while.10 = (s32[]{:T(128)}, f32[8,16,64,128]{3,2,1,0:T(8,128)}, f32[8,48,16,32]{1,3,2,0:T(8,128)}, f32[48,64,32]{1,0,2:T(8,128)S(1)}, f32[1024,128]{1,0:T(8,128)S(1)}, /*index=5*/s32[]{:T(128)}) while((s32[]{:T(128)}, f32[8,16,64,128]{3,2,1,0:T(8,128)}, f32[8,48,16,32]{1,3,2,0:T(8,128)}, f32[48,64,32]{1,0,2:T(8,128)S(1)}, ...), condition=%wide.region_6.7_spmd, body=%wide.region_5.6_spmd.sunk | while | flops 2215641088 | bytes 18482244 | solution.py:87
  157.0 8.1 %multiply_bitcast_fusion.2 = f32[16,64,32,32]{1,2,3,0:T(8,128)S(1)} fusion(f32[48,64,32]{1,0,2:T(8,128)S(1)} %get-tuple-element.111, f32[8,48,16,32]{1,3,2,0:T(8,128)} %get-tuple-element.110, s32[]{:T(128)} %get-tuple-element.102), kind=kOutput, calls=%fused_computation.clone.1 | convolution fusion | flops 605028352 | bytes 4850176 | tf_op jit(solution)/shard_map/while/body/eval_jaxpr/sic,sje->ijce/dot_general | solution.py:79
  165.1 6.5 %copy.77 = f32[16,64,32,32]{1,3,2,0:T(8,128)S(1)} copy(f32[16,64,32,32]{1,2,3,0:T(8,128)S(1)} %multiply_bitcast_fusion.2) | data formatting | bytes 8388608 | tf_op jit(solution)/shard_map/while/body/eval_jaxpr/div | solution.py:79
  171.6 14.1 %fusion.69 = f32[8,16,64,128]{3,2,1,0:T(8,128)} fusion(f32[8,16,64,128]{3,2,1,0:T(8,128)} %get-tuple-element.103, s32[]{:T(128)} %get-tuple-element.102, f32[16,64,1024]{1,2,0:T(8,128)S(1)} %bitcast.92, f32[1024,128]{1,0:T(8,128)S(1)} %get-tuple-element.112), kind=kOutput, calls=%fused_computation.2.clone.1 | convolution fusion | flops 1610612736 | bytes 5243392 | tf_op jit(solution)/shard_map/while/body/eval_jaxpr/dot_general | solution.py:83
  185.7 8.1 %multiply_bitcast_fusion.2 = f32[16,64,32,32]{1,2,3,0:T(8,128)S(1)} fusion(f32[48,64,32]{1,0,2:T(8,128)S(1)} %get-tuple-element.111, f32[8,48,16,32]{1,3,2,0:T(8,128)} %get-tuple-element.110, s32[]{:T(128)} %get-tuple-element.102), kind=kOutput, calls=%fused_computation.clone.1 | convolution fusion | flops 605028352 | bytes 4850176 | tf_op jit(solution)/shard_map/while/body/eval_jaxpr/sic,sje->ijce/dot_general | solution.py:79
  193.8 6.5 %copy.77 = f32[16,64,32,32]{1,3,2,0:T(8,128)S(1)} copy(f32[16,64,32,32]{1,2,3,0:T(8,128)S(1)} %multiply_bitcast_fusion.2) | data formatting | bytes 8388608 | tf_op jit(solution)/shard_map/while/body/eval_jaxpr/div | solution.py:79
  200.3 14.1 %fusion.69 = f32[8,16,64,128]{3,2,1,0:T(8,128)} fusion(f32[8,16,64,128]{3,2,1,0:T(8,128)} %get-tuple-element.103, s32[]{:T(128)} %get-tuple-element.102, f32[16,64,1024]{1,2,0:T(8,128)S(1)} %bitcast.92, f32[1024,128]{1,0:T(8,128)S(1)} %get-tuple-element.112), kind=kOutput, calls=%fused_computation.2.clone.1 | convolution fusion | flops 1610612736 | bytes 5243392 | tf_op jit(solution)/shard_map/while/body/eval_jaxpr/dot_general | solution.py:83
  214.4 8.1 %multiply_bitcast_fusion.2 = f32[16,64,32,32]{1,2,3,0:T(8,128)S(1)} fusion(f32[48,64,32]{1,0,2:T(8,128)S(1)} %get-tuple-element.111, f32[8,48,16,32]{1,3,2,0:T(8,128)} %get-tuple-element.110, s32[]{:T(128)} %get-tuple-element.102), kind=kOutput, calls=%fused_computation.clone.1 | convolution fusion | flops 605028352 | bytes 4850176 | tf_op jit(solution)/shard_map/while/body/eval_jaxpr/sic,sje->ijce/dot_general | solution.py:79
  222.5 6.5 %copy.77 = f32[16,64,32,32]{1,3,2,0:T(8,128)S(1)} copy(f32[16,64,32,32]{1,2,3,0:T(8,128)S(1)} %multiply_bitcast_fusion.2) | data formatting | bytes 8388608 | tf_op jit(solution)/shard_map/while/body/eval_jaxpr/div | solution.py:79
  229.0 14.1 %fusion.69 = f32[8,16,64,128]{3,2,1,0:T(8,128)} fusion(f32[8,16,64,128]{3,2,1,0:T(8,128)} %get-tuple-element.103, s32[]{:T(128)} %get-tuple-element.102, f32[16,64,1024]{1,2,0:T(8,128)S(1)} %bitcast.92, f32[1024,128]{1,0:T(8,128)S(1)} %get-tuple-element.112), kind=kOutput, calls=%fused_computation.2.clone.1 | convolution fusion | flops 1610612736 | bytes 5243392 | tf_op jit(solution)/shard_map/while/body/eval_jaxpr/dot_general | solution.py:83
  243.1 8.1 %multiply_bitcast_fusion.2 = f32[16,64,32,32]{1,2,3,0:T(8,128)S(1)} fusion(f32[48,64,32]{1,0,2:T(8,128)S(1)} %get-tuple-element.111, f32[8,48,16,32]{1,3,2,0:T(8,128)} %get-tuple-element.110, s32[]{:T(128)} %get-tuple-element.102), kind=kOutput, calls=%fused_computation.clone.1 | convolution fusion | flops 605028352 | bytes 4850176 | tf_op jit(solution)/shard_map/while/body/eval_jaxpr/sic,sje->ijce/dot_general | solution.py:79
  251.2 6.5 %copy.77 = f32[16,64,32,32]{1,3,2,0:T(8,128)S(1)} copy(f32[16,64,32,32]{1,2,3,0:T(8,128)S(1)} %multiply_bitcast_fusion.2) | data formatting | bytes 8388608 | tf_op jit(solution)/shard_map/while/body/eval_jaxpr/div | solution.py:79
  257.7 14.1 %fusion.69 = f32[8,16,64,128]{3,2,1,0:T(8,128)} fusion(f32[8,16,64,128]{3,2,1,0:T(8,128)} %get-tuple-element.103, s32[]{:T(128)} %get-tuple-element.102, f32[16,64,1024]{1,2,0:T(8,128)S(1)} %bitcast.92, f32[1024,128]{1,0:T(8,128)S(1)} %get-tuple-element.112), kind=kOutput, calls=%fused_computation.2.clone.1 | convolution fusion | flops 1610612736 | bytes 5243392 | tf_op jit(solution)/shard_map/while/body/eval_jaxpr/dot_general | solution.py:83
  271.8 8.1 %multiply_bitcast_fusion.2 = f32[16,64,32,32]{1,2,3,0:T(8,128)S(1)} fusion(f32[48,64,32]{1,0,2:T(8,128)S(1)} %get-tuple-element.111, f32[8,48,16,32]{1,3,2,0:T(8,128)} %get-tuple-element.110, s32[]{:T(128)} %get-tuple-element.102), kind=kOutput, calls=%fused_computation.clone.1 | convolution fusion | flops 605028352 | bytes 4850176 | tf_op jit(solution)/shard_map/while/body/eval_jaxpr/sic,sje->ijce/dot_general | solution.py:79
  279.9 6.5 %copy.77 = f32[16,64,32,32]{1,3,2,0:T(8,128)S(1)} copy(f32[16,64,32,32]{1,2,3,0:T(8,128)S(1)} %multiply_bitcast_fusion.2) | data formatting | bytes 8388608 | tf_op jit(solution)/shard_map/while/body/eval_jaxpr/div | solution.py:79
  286.4 14.1 %fusion.69 = f32[8,16,64,128]{3,2,1,0:T(8,128)} fusion(f32[8,16,64,128]{3,2,1,0:T(8,128)} %get-tuple-element.103, s32[]{:T(128)} %get-tuple-element.102, f32[16,64,1024]{1,2,0:T(8,128)S(1)} %bitcast.92, f32[1024,128]{1,0:T(8,128)S(1)} %get-tuple-element.112), kind=kOutput, calls=%fused_computation.2.clone.1 | convolution fusion | flops 1610612736 | bytes 5243392 | tf_op jit(solution)/shard_map/while/body/eval_jaxpr/dot_general | solution.py:83
  300.5 8.1 %multiply_bitcast_fusion.2 = f32[16,64,32,32]{1,2,3,0:T(8,128)S(1)} fusion(f32[48,64,32]{1,0,2:T(8,128)S(1)} %get-tuple-element.111, f32[8,48,16,32]{1,3,2,0:T(8,128)} %get-tuple-element.110, s32[]{:T(128)} %get-tuple-element.102), kind=kOutput, calls=%fused_computation.clone.1 | convolution fusion | flops 605028352 | bytes 4850176 | tf_op jit(solution)/shard_map/while/body/eval_jaxpr/sic,sje->ijce/dot_general | solution.py:79
  308.6 6.5 %copy.77 = f32[16,64,32,32]{1,3,2,0:T(8,128)S(1)} copy(f32[16,64,32,32]{1,2,3,0:T(8,128)S(1)} %multiply_bitcast_fusion.2) | data formatting | bytes 8388608 | tf_op jit(solution)/shard_map/while/body/eval_jaxpr/div | solution.py:79
  315.1 14.1 %fusion.69 = f32[8,16,64,128]{3,2,1,0:T(8,128)} fusion(f32[8,16,64,128]{3,2,1,0:T(8,128)} %get-tuple-element.103, s32[]{:T(128)} %get-tuple-element.102, f32[16,64,1024]{1,2,0:T(8,128)S(1)} %bitcast.92, f32[1024,128]{1,0:T(8,128)S(1)} %get-tuple-element.112), kind=kOutput, calls=%fused_computation.2.clone.1 | convolution fusion | flops 1610612736 | bytes 5243392 | tf_op jit(solution)/shard_map/while/body/eval_jaxpr/dot_general | solution.py:83
  329.2 8.1 %multiply_bitcast_fusion.2 = f32[16,64,32,32]{1,2,3,0:T(8,128)S(1)} fusion(f32[48,64,32]{1,0,2:T(8,128)S(1)} %get-tuple-element.111, f32[8,48,16,32]{1,3,2,0:T(8,128)} %get-tuple-element.110, s32[]{:T(128)} %get-tuple-element.102), kind=kOutput, calls=%fused_computation.clone.1 | convolution fusion | flops 605028352 | bytes 4850176 | tf_op jit(solution)/shard_map/while/body/eval_jaxpr/sic,sje->ijce/dot_general | solution.py:79
  337.3 6.5 %copy.77 = f32[16,64,32,32]{1,3,2,0:T(8,128)S(1)} copy(f32[16,64,32,32]{1,2,3,0:T(8,128)S(1)} %multiply_bitcast_fusion.2) | data formatting | bytes 8388608 | tf_op jit(solution)/shard_map/while/body/eval_jaxpr/div | solution.py:79
  343.8 14.1 %fusion.69 = f32[8,16,64,128]{3,2,1,0:T(8,128)} fusion(f32[8,16,64,128]{3,2,1,0:T(8,128)} %get-tuple-element.103, s32[]{:T(128)} %get-tuple-element.102, f32[16,64,1024]{1,2,0:T(8,128)S(1)} %bitcast.92, f32[1024,128]{1,0:T(8,128)S(1)} %get-tuple-element.112), kind=kOutput, calls=%fused_computation.2.clone.1 | convolution fusion | flops 1610612736 | bytes 5243392 | tf_op jit(solution)/shard_map/while/body/eval_jaxpr/dot_general | solution.py:83
  357.9 8.1 %multiply_bitcast_fusion.2 = f32[16,64,32,32]{1,2,3,0:T(8,128)S(1)} fusion(f32[48,64,32]{1,0,2:T(8,128)S(1)} %get-tuple-element.111, f32[8,48,16,32]{1,3,2,0:T(8,128)} %get-tuple-element.110, s32[]{:T(128)} %get-tuple-element.102), kind=kOutput, calls=%fused_computation.clone.1 | convolution fusion | flops 605028352 | bytes 4850176 | tf_op jit(solution)/shard_map/while/body/eval_jaxpr/sic,sje->ijce/dot_general | solution.py:79
  366.0 6.5 %copy.77 = f32[16,64,32,32]{1,3,2,0:T(8,128)S(1)} copy(f32[16,64,32,32]{1,2,3,0:T(8,128)S(1)} %multiply_bitcast_fusion.2) | data formatting | bytes 8388608 | tf_op jit(solution)/shard_map/while/body/eval_jaxpr/div | solution.py:79
  372.5 14.1 %fusion.69 = f32[8,16,64,128]{3,2,1,0:T(8,128)} fusion(f32[8,16,64,128]{3,2,1,0:T(8,128)} %get-tuple-element.103, s32[]{:T(128)} %get-tuple-element.102, f32[16,64,1024]{1,2,0:T(8,128)S(1)} %bitcast.92, f32[1024,128]{1,0:T(8,128)S(1)} %get-tuple-element.112), kind=kOutput, calls=%fused_computation.2.clone.1 | convolution fusion | flops 1610612736 | bytes 5243392 | tf_op jit(solution)/shard_map/while/body/eval_jaxpr/dot_general | solution.py:83
  386.6 0.0 reduce-scatter.2.cloned.1.call-start
  386.7 3.2 slice.8
  389.9 4.1 copy.38
  394.0 20.9 %all-reduce.5.cloned.1.call-done = f32[128,64,128]{2,1,0:T(8,128)} async-done(((f32[128,64,128]{2,1,0:T(8,128)}), f32[128,64,128]{2,1,0:T(8,128)}) %all-reduce.5.cloned.1.call-update) | async-done | bytes 4194320 | tf_op jit(solution)/shard_map/psum | solution.py:88
  414.9 4.6 fusion.57
  419.5 2.7 multiply_reduce_fusion
  422.3 12.4 %fusion.58 = (f32[128,8]{1,0:T(8,128)S(1)}, f32[128,8,64]{2,1,0:T(8,128)S(1)}) fusion(f32[128,8]{0,1:T(8,128)S(1)} %copy-done.10, f32[128,64,128]{2,1,0:T(8,128)S(1)} %get-tuple-element.62, f32[128,64]{1,0:T(8,128)S(1)} %add_sqrt_fusion, f32[128,64]{1,0:T(8,128)S(1)} %broadcast_multiply_fusion), kind=kOutput, calls=%fused_computation.72 | convolution fusion | flops 102824960 | bytes 4530176 | tf_op jit(solution)/shard_map/ijc,ch->ihj/dot_general | solution.py:22
  434.8 19.9 %pmax.7 = f32[128,8]{1,0:T(8,128)S(1)} all-reduce(f32[128,8]{1,0:T(8,128)S(1)} %get-tuple-element.63), channel_id=1, replica_groups=mesh['grp'=2,'col'=4,'row'=2,'seq'=2] {'col'}, use_global_device_ids=true, to_apply=%region_11.12 | all-reduce | flops 1024 | bytes 8192 | tf_op jit(solution)/shard_map/pmax | solution.py:91
  454.7 0.4 fusion.46
  455.0 16.7 %psum.23 = f32[128,8]{1,0:T(8,128)S(1)} all-reduce(f32[128,8]{1,0:T(8,128)S(1)} %fusion.46), channel_id=1, replica_groups=mesh['grp'=2,'col'=4,'row'=2,'seq'=2] {'col'}, use_global_device_ids=true, to_apply=%region_13.14 | all-reduce | flops 1024 | bytes 8192 | tf_op jit(solution)/shard_map/psum | solution.py:92
  471.8 0.3 divide_bitcast_fusion
  472.1 8.1 %fusion.16 = f32[48,128,8,32]{1,3,0,2:T(8,128)S(1)} fusion(f32[48,64,8,32]{1,3,2,0:T(8,128)} %bitcast.93, f32[128,8,64,1]{2,1,0,3:T(8,128)S(1)} %divide_bitcast_fusion), kind=kOutput, calls=%fused_computation.20 | convolution fusion | flops 1207959552 | bytes 9699328 | tf_op jit(solution)/shard_map/ihj,sjhd->sihd/dot_general | solution.py:94
  480.2 3.4 copy.45
  483.6 6.7 %copy.46 = f32[48,128,256]{2,0,1:T(8,128)} copy(f32[48,128,256]{1,2,0:T(8,128)} %bitcast.94) | data formatting | bytes 12582912 | tf_op jit(solution)/shard_map/reshape | solution.py:96
  490.3 1.1 copy-done.6
  491.4 0.3 reduce_sum.88
  491.7 0.5 multiply_reduce_fusion.2
  492.2 1.5 fusion.40
  493.7 106.8 %reduce-scatter.2.cloned.1.call-done = f32[48,32,256]{2,0,1:T(8,128)} async-done(((f32[48,128,256]{2,0,1:T(8,128)}), f32[48,32,256]{2,0,1:T(8,128)}) %reduce-scatter.2.cloned.1.call-update) | async-done | bytes 1572880 | tf_op jit(solution)/shard_map/reduce_scatter | solution.py:97
  600.5 4.5 fusion.36
  (32 shorter events, 0.2 us)
Async XLA Ops:
  7.2 485.0 %copy-start = (f32[64,256]{1,0:T(8,128)S(1)}, f32[64,256]{1,0:T(8,128)}, u32[]{:S(2)}) copy-start(f32[64,256]{1,0:T(8,128)} %param.18) | copy-start | bytes 196612
  7.2 68.6 %all-gather.2.cloned.1.call-start = ((), (), s32[]{:S(2)}) async-start(), calls=%async_computation.1 | async-start | bytes 3932160 | tf_op jit(solution)/shard_map/all_gather | solution.py:48
  7.9 121.1 %all-reduce.3.cloned.1.call-start = ((), (), s32[]{:S(2)}) async-start(), calls=%async_computation.2 | async-start | bytes 3145728 | tf_op jit(solution)/shard_map/psum | solution.py:12
  75.8 3.0 copy-start.1
  78.7 3.0 copy-start.9
  78.7 336.2 %all-reduce.5.cloned.1.call-start = ((), (), s32[]{:S(2)}) async-start(), calls=%async_computation.3 | async-start | bytes 8388608 | tf_op jit(solution)/shard_map/psum | solution.py:88
  93.9 39.5 %copy-start.7 = (f32[64,256]{1,0:T(8,128)S(1)}, f32[64,256]{1,0:T(8,128)}, u32[]{:S(2)}) copy-start(f32[64,256]{1,0:T(8,128)} %param.17) | copy-start | bytes 196612
  129.0 4.4 copy-start.4
  138.1 2.1 copy-start.2
  140.2 1.0 copy-start.5
  386.6 213.9 %reduce-scatter.2.cloned.1.call-start = ((), (), s32[]{:S(2)}) async-start(), calls=%async_computation.4 | async-start | bytes 7864320 | tf_op jit(solution)/shard_map/reduce_scatter | solution.py:97
  419.5 15.2 %copy-start.3 = (f32[128,64,128]{2,1,0:T(8,128)}, f32[128,64,128]{2,1,0:T(8,128)S(1)}, u32[]{:S(2)}) copy-start(f32[128,64,128]{2,1,0:T(8,128)S(1)} %get-tuple-element.62) | copy-start | bytes 12582916
  419.5 2.8 copy-start.10
  490.2 1.1 copy-start.6
  491.4 109.1 %copy-start.8 = (f32[256,64]{0,1:T(8,128)S(1)}, f32[256,64]{0,1:T(8,128)}, u32[]{:S(2)}) copy-start(f32[256,64]{0,1:T(8,128)} %param.19) | copy-start | bytes 196612
Sparse Core Ops, SparseCore 0:
  9.6 66.1 all-gather.1
  78.8 50.1 all-reduce.2
  386.8 28.0 all-reduce.4
  490.4 110.0 reduce-scatter.1
where the time goes:
time: 620 us; the launch traced here: 612 us
  waiting for transfers between devices  231 us (37%)
  matrix products  221 us (36%)
  local copies, waits for them, and re-layouts  74.5 us (12%)
  blocking collectives  36.6 us (6%)
  other arithmetic  18.9 us (3%)
  loops' own time  15.9 us (3%)
  between operations  14.3 us (2%)
    dot_general x8, matrix products, outer_block(): jnp.dot(flat_prod, tensor_product_matrix, precision=exact_arithmetic)  113 us
    reduce_scatter x1, waiting for transfers between devices, on_device(): lax.psum_scatter(mixed_rows, 'col', scatter_dimension=1, tiled=True)  107 us
    all_gather x1, waiting for transfers between devices, on_device(): gathered_lines = lax.all_gather(alignment_tensor, 'col', axis=2, tiled=True)  67 us
    dot_general x8, matrix products, outer_block(): jnp.einsum('sic,sje->ijce', left_block, second_factor_tile, precision=exa...  64.7 us
    div x8, local copies, waits for them, and re-layouts, outer_block(): jnp.einsum('sic,sje->ijce', left_block, second_factor_tile, precision=exa...  51.9 us
    psum x1, waiting for transfers between devices, broadcast(): return lax.psum(block, axis)  35.1 us
    psum x1, waiting for transfers between devices, on_device(): revised_couplings = residue_couplings + lax.psum(update, 'seq')  20.9 us
    pmax x1, blocking collectives, on_device(): score_top = lax.pmax(local_top, 'col')  19.9 us
  transfers between devices with their start and end apart: 4, of which 4 were waited for; matrix products, arithmetic and copies ran while one was open for 4% of the time, Pallas kernels for 0%

commit v1 on v0

--- a/solution.py
+++ b/solution.py
@@ -1,6 +1,10 @@
+import functools
+
 import jax
 import jax.numpy as jnp
 from jax import lax
+from jax.experimental import pallas as pl
+from jax.experimental.pallas import tpu as pltpu
 from jax.sharding import PartitionSpec as P
 
 epsilon = 1e-05
@@ -27,7 +31,7 @@
     )
 
 
-def on_device(
+def general_path(
     alignment_tensor,
     residue_couplings,
     first_factor_matrix,
@@ -110,6 +114,243 @@
     return (revised_alignment, revised_couplings)
 
 
+f32, bf16 = jnp.float32, jnp.bfloat16
+LANES = 128
+
+
+def halves(values):
+    high = values.astype(bf16)
+    return high, (values - high.astype(f32)).astype(bf16)
+
+
+def mm(a, b):
+    return jnp.dot(a, b, preferred_element_type=f32)
+
+
+def mm3(a, b):
+    (a_high, a_low), (b_high, b_low) = a, b
+    return mm(a_high, b_high) + (mm(a_high, b_low) + mm(a_low, b_high))
+
+
+def pair_kernel(
+    depth, part_ref, left_ref, right_ref, product_ref, score_ref, pair_ref, out_ref, scores_ref, high_ref, low_ref
+):
+    width = high_ref.shape[0]
+    rows = high_ref.shape[2]
+    own_cols = scores_ref.shape[0]
+    all_cols = pair_ref.shape[0] // rows
+    outer = right_ref.shape[0] // own_cols
+    r_high, r_low = halves(right_ref[...])
+    r_both = jnp.concatenate([r_high, r_low], axis=1)
+
+    def first(step, carry):
+        start = pl.multiple_of(step * 2 * rows, 2 * rows)
+        l_high, l_low = halves(left_ref[:, pl.ds(start, 2 * rows)])
+        product = mm(r_both, jnp.concatenate([l_high, l_high], axis=0)) + mm(r_high, l_low)
+        p_high, p_low = halves(product)
+        for t in range(2):
+            high_ref[2 * step + t] = p_high[:, t * rows : (t + 1) * rows]
+            low_ref[2 * step + t] = p_low[:, t * rows : (t + 1) * rows]
+        return carry
+
+    lax.fori_loop(0, width // 2, first, 0)
+    t_high, t_low = halves(product_ref[...])
+    channels = t_high.shape[0]
+    t_both = jnp.concatenate([t_high, t_low], axis=0)
+    c_halves = halves(score_ref[...])
+    first_col = part_ref[0] * own_cols
+
+    def second(step, carry):
+        def block(ref):
+            pieces = [
+                ref[:, pl.ds(pl.multiple_of((2 * step + t) * outer, outer), outer), :].reshape(width * outer, rows)
+                for t in range(2)
+            ]
+            return jnp.concatenate(pieces, axis=1)
+
+        both = mm(t_both, block(high_ref))
+        update = (both[:channels] + (both[channels:] + mm(t_high, block(low_ref)))) / depth
+        for t in range(2):
+            col = 2 * step + t
+            pair = pair_ref[pl.ds(first_col + col, rows, stride=all_cols), :].T
+            revised = pair + update[:, t * rows : (t + 1) * rows]
+            out_ref[pl.ds(col, rows, stride=own_cols), :] = revised.T
+            center = revised - jnp.mean(revised, axis=0, keepdims=True)
+            spread = jnp.mean(center * center, axis=0, keepdims=True)
+            normed = center / jnp.sqrt(spread + epsilon)
+            scores_ref[col] = mm3(c_halves, halves(normed))
+        return carry
+
+    lax.fori_loop(0, own_cols // 2, second, 0)
+
+
+def mix_kernel(
+    heads, weights_ref, normed_ref, own_ref, raw_ref, source_ref, gate_ref, final_ref, out_ref, mixed_ref
+):
+    groups = normed_ref.shape[1]
+    tokens = normed_ref.shape[0] * normed_ref.shape[2]
+    own = own_ref.shape[1]
+    wide = source_ref.shape[1]
+    w_high, w_low = halves(weights_ref[...])
+    w_both = jnp.concatenate([w_high, w_low], axis=0)
+    entries = w_high.shape[0]
+    s_high, s_low = halves(source_ref[...])
+    s_twice = jnp.concatenate([s_high, s_high], axis=0)
+    row_head = lax.broadcasted_iota(jnp.int32, (entries, wide), 0) // own
+    lane_head = lax.broadcasted_iota(jnp.int32, (entries, wide), 1) // (wide // 2 // heads) % heads
+    mask = row_head == lane_head
+
+    def step(group, carry):
+        x_high, x_low = halves(normed_ref[:, group].reshape(tokens, LANES))
+        values = mm(jnp.concatenate([x_high, x_low], axis=1), s_twice) + mm(x_high, s_low)
+        v_high, v_low = halves(values)
+        both = mm(w_both, v_high)
+        full = both[:entries] + (both[entries:] + mm(w_high, v_low))
+        kept = jnp.where(mask, full, 0.0)
+        mixed_ref[group] = jnp.sum(kept.reshape(heads, own, wide), axis=0)
+        return carry
+
+    lax.fori_loop(0, groups, step, 0)
+    g_halves = halves(gate_ref[...])
+    f_halves = halves(final_ref[...])
+
+    def finish(chunk, carry):
+        at = pl.ds(chunk * (groups // 3), groups // 3)
+        own_rows = own_ref[at].reshape(-1, LANES)
+        gates = jax.nn.sigmoid(mm3(halves(own_rows), g_halves))
+        gated = gates * mixed_ref[at].reshape(-1, wide)
+        out = raw_ref[at].reshape(-1, LANES) + mm3(halves(gated), f_halves)
+        out_ref[at] = out.reshape(groups // 3, own, LANES)
+        return carry
+
+    lax.fori_loop(0, 3, finish, 0)
+
+
+def twice(matrix):
+    zero = jnp.zeros_like(matrix)
+    return jnp.concatenate(
+        [jnp.concatenate([matrix, zero], axis=1), jnp.concatenate([zero, matrix], axis=1)], axis=0
+    )
+
+
+def pack(values):
+    half = values.shape[0] // 2
+    return jnp.concatenate([values[:half], values[half:]], axis=-1)
+
+
+def whole_vmem(count):
+    return [pl.BlockSpec(memory_space=pltpu.VMEM)] * count
+
+
+def fast_path(
+    alignment_tensor,
+    residue_couplings,
+    first_factor_matrix,
+    second_factor_matrix,
+    tensor_product_matrix,
+    coupling_score_matrix,
+    averaged_source_matrix,
+    sigmoid_matrix,
+    final_matrix,
+):
+    seqs, _, own, depth = alignment_tensor.shape
+    rows, cols, channels = residue_couplings.shape
+    outer = first_factor_matrix.shape[1]
+    heads = coupling_score_matrix.shape[1]
+    row_size, col_size, seq_size = (lax.axis_size(a) for a in ("row", "col", "seq"))
+    total = seqs * seq_size
+    blocks = row_size * col_size
+    half_cols = cols // seq_size
+    row, col, seq = (lax.axis_index(a) for a in ("row", "col", "seq"))
+
+    raw = alignment_tensor.reshape(seqs, own, depth)
+    normed = pack(standardize_entries(raw))
+    gathered = lax.all_gather(normed, ("row", "col"), axis=0, tiled=False)
+
+    def project(block, matrix):
+        both = jnp.einsum("pstk,kc->pstc", block, twice(matrix), precision=lax.Precision.HIGH)
+        return both.reshape(both.shape[:3] + (2, outer))
+
+    left = project(lax.dynamic_slice_in_dim(gathered, row * col_size, col_size, 0), first_factor_matrix)
+    left = left.transpose(3, 1, 4, 0, 2).reshape(seqs, outer * rows)
+    right = project(lax.dynamic_slice_in_dim(gathered, col * seq_size, seq_size, 0), second_factor_matrix)
+    right = right.transpose(0, 3, 1, 2, 4).reshape(seq_size, seqs, half_cols * outer)
+    left_all = lax.all_gather(left, "seq", axis=0, tiled=True)
+    right_all = lax.all_to_all(right, "seq", 0, 0, tiled=True).reshape(total, half_cols * outer)
+    room = -total % LANES
+    left_all = jnp.pad(left_all, ((0, room), (0, 0)))
+    right_all = jnp.pad(right_all, ((0, room), (0, 0))).T
+
+    revised, scores = pl.pallas_call(
+        functools.partial(pair_kernel, total),
+        out_shape=(
+            jax.ShapeDtypeStruct((rows * half_cols, channels), f32),
+            jax.ShapeDtypeStruct((half_cols, heads, rows), f32),
+        ),
+        in_specs=[pl.BlockSpec(memory_space=pltpu.SMEM)] + whole_vmem(5),
+        out_specs=tuple(whole_vmem(2)),
+        scratch_shapes=[pltpu.VMEM((outer, half_cols * outer, rows), bf16)] * 2,
+        compiler_params=pltpu.CompilerParams(vmem_limit_bytes=56 << 20),
+    )(
+        seq.astype(jnp.int32).reshape(1),
+        left_all,
+        right_all,
+        tensor_product_matrix.T,
+        coupling_score_matrix.T,
+        residue_couplings.reshape(rows * cols, channels),
+    )
+    revised_couplings = lax.all_gather(revised.reshape(rows, half_cols, channels), "seq", axis=1, tiled=True)
+
+    parted = scores.reshape(half_cols, heads, col_size, own).transpose(2, 1, 3, 0)
+    parted = jnp.broadcast_to(
+        parted[:, None], (col_size, seq_size, heads, own, half_cols)
+    ).reshape(col_size * seq_size, heads * own, half_cols)
+    received = lax.all_to_all(parted, ("col", "seq"), 0, 0, tiled=True)
+    received = received.transpose(1, 0, 2).reshape(heads * own, col_size * seq_size * half_cols)
+    weights = jax.nn.softmax(received, axis=-1)
+
+    groups = seqs // 2
+    wide = 2 * averaged_source_matrix.shape[1]
+    packed = pl.pallas_call(
+        functools.partial(mix_kernel, heads),
+        out_shape=jax.ShapeDtypeStruct((groups, own, LANES), f32),
+        in_specs=whole_vmem(7),
+        out_specs=whole_vmem(1)[0],
+        scratch_shapes=[pltpu.VMEM((groups, own, wide), f32)],
+        compiler_params=pltpu.CompilerParams(vmem_limit_bytes=56 << 20),
+    )(
+        weights,
+        gathered,
+        normed,
+        pack(raw),
+        twice(averaged_source_matrix),
+        twice(sigmoid_matrix),
+        twice(final_matrix),
+    )
+    revised_alignment = jnp.concatenate([packed[..., :depth], packed[..., depth:]], axis=0)
+    return revised_alignment.reshape(alignment_tensor.shape), revised_couplings
+
+
+def on_device(alignment_tensor, residue_couplings, first_factor_matrix, *rest):
+    seqs, tiles, own, depth = alignment_tensor.shape
+    rows, cols, channels = residue_couplings.shape
+    row_size, col_size, seq_size = (lax.axis_size(a) for a in ("row", "col", "seq"))
+    fits = (
+        tiles == 1
+        and rows == own * col_size == LANES
+        and cols == own * seq_size
+        and row_size * rows == col_size * cols
+        and own % 16 == 0
+        and seqs % 6 == 0
+        and 2 * depth == channels == LANES
+        and first_factor_matrix.shape[1] % 16 == 0
+        and seq_size == 2
+        and seqs * seq_size <= LANES
+    )
+    path = fast_path if fits else general_path
+    return path(alignment_tensor, residue_couplings, first_factor_matrix, *rest)
+
+
 def solution(mesh):
     return jax.shard_map(
         on_device,

time: 620 us -> 179 us (0.29); the launches traced: 612 us -> 179 us
  matrix products: 221 us -> 5.06 us
  waiting for transfers between devices: 231 us -> 70.8 us
  local copies, waits for them, and re-layouts: 74.5 us -> 27.5 us
  Pallas kernels: 0 us -> 43.4 us
  blocking collectives: 36.6 us -> 4.19 us
  loops' own time: 15.9 us -> 0 us
  other arithmetic: 18.9 us -> 10.1 us
    dot_general x22 -> x2, matrix products: 221 us -> 5.06 us  [project(): jnp.einsum('pstk,kc->pstc', block, twice(matrix), precision=lax.Precision...]
    reduce_scatter x1 -> x0, waiting for transfers between devices: 107 us -> none  [on_device(): lax.psum_scatter(mixed_rows, 'col', scatter_dimension=1, tiled=True)]
    psum x2 -> x0, waiting for transfers between devices: 56 us -> none  [the longest x1 35.1 us: broadcast(): return lax.psum(block, axis)]
    div x9 -> x0, local copies, waits for them, and re-layouts: 52 us -> none  [the longest x8 51.9 us: outer_block(): jnp.einsum('sic,sje->ijce', left_block, second_factor_tile, precision=exa...]
    pallas_call x0 -> x2, Pallas kernels: none -> 43.4 us  [the longest x1 23.1 us: fast_path(): pl.pallas_call(functools.partial(pair_kernel, total), out_shape=(jax.Shap...]
    pmax x1 -> x0, blocking collectives: 19.9 us -> none  [on_device(): score_top = lax.pmax(local_top, 'col')]
    psum x1 -> x0, blocking collectives: 16.7 us -> none  [on_device(): lax.psum(jnp.sum(jnp.exp(scores - score_top[:, :, None]), axis=2), 'col')]
    another operation x1 -> x0, loops' own time: 15.9 us -> none  [on_device(): lax.map(outer_block, left_blocks).reshape(coupling_lines, col_count, -1)]
  transfers between devices with their start and end apart: 4 -> 4, of which waited for: 4 -> 2; matrix products, arithmetic and copies ran while one was open for 4% -> 8% of each run, Pallas kernels for 0% -> 11%
where the time goes in v1:
time: 179 us
  waiting for transfers between devices  70.8 us (40%)
  Pallas kernels  43.4 us (24%)
  local copies, waits for them, and re-layouts  27.5 us (15%)
  between operations  13.9 us (8%)
  other arithmetic  10.1 us (6%)
  matrix products  5.06 us (3%)
  blocking collectives  4.19 us (2%)
  starting transfers between devices  3.82 us (2%)
    all_gather x1, waiting for transfers between devices, fast_path(): gathered = lax.all_gather(normed, ('row', 'col'), axis=0, tiled=False)  62.8 us
    pallas_call x1, Pallas kernels, fast_path(): pl.pallas_call(functools.partial(pair_kernel, total), out_shape=(jax.Shap...  23.1 us
    pallas_call x1, Pallas kernels, fast_path(): pl.pallas_call(functools.partial(mix_kernel, heads), out_shape=jax.ShapeD...  20.4 us
    all_to_all x1, waiting for transfers between devices, fast_path(): received = lax.all_to_all(parted, ('col', 'seq'), 0, 0, tiled=True)  7.86 us
    reshape x4, local copies, waits for them, and re-layouts, project(): return both.reshape(both.shape[:3] + (2, outer))  7.66 us
    unnamed x17, local copies, waits for them, and re-layouts  5.91 us
    reshape x1, local copies, waits for them, and re-layouts, fast_path(): left = left.transpose(3, 1, 4, 0, 2).reshape(seqs, outer * rows)  5.36 us
    dot_general x2, matrix products, project(): jnp.einsum('pstk,kc->pstc', block, twice(matrix), precision=lax.Precision...  5.06 us
  transfers between devices with their start and end apart: 4, of which 2 were waited for; matrix products, arithmetic and copies ran while one was open for 8% of the time, Pallas kernels for 11%

profile of v1, /device:TPU:0, one launch (start us, length us, event | category | flops | bytes accessed | tf_op | source)
XLA Modules:
  0.0 178.8 jit_solution(16269507858810402448)
XLA Ops:
  7.2 0.0 copy-start.5
  7.2 0.0 all-gather.9.cloned.1.call-start
  7.2 1.4 reduce_sum.27
  8.6 1.6 multiply_reduce_fusion
  10.3 1.6 fusion.4
  11.9 0.1 fusion.29
  12.0 0.9 pad_maximum_fusion.own_ref
  12.9 0.0 all-gather.9.cloned.1.call-update
  12.9 0.0 all-gather.5.cloned.1.call-start
  13.0 62.8 %all-gather.9.cloned.1.call-done = f32[192,32,128]{2,1,0:T(8,128)} async-done(((f32[24,32,128]{2,1,0:T(8,128)}), f32[192,32,128]{2,1,0:T(8,128)}) %all-gather.9.cloned.1.call-update) | async-done | bytes 3145744 | tf_op jit(solution)/shard_map/all_gather | solution.py:268
  75.8 0.0 copy-done.5
  75.8 3.4 %fusion = f32[4,24,32,64]{3,2,1,0:T(8,128)} fusion(f32[8,24,32,128]{3,2,1,0:T(8,128)} %bitcast.60, s32[]{:T(128)S(6)} %select_n.6, f32[64,32]{0,1:T(8,128)S(1)} %copy-done.5), kind=kOutput, calls=%fused_computation.1 | convolution fusion | flops 151035904 | bytes 2367492 | tf_op jit(solution)/shard_map/pstk,kc->pstc/dot_general | solution.py:271
  79.2 3.2 %reshape.66 = f32[4,24,32,2,32]{4,3,2,1,0:T(2,128)S(1)} reshape(f32[4,24,32,64]{3,2,1,0:T(8,128)} %fusion) | data formatting | bytes 1572864 | tf_op jit(solution)/shard_map/reshape | solution.py:272
  82.4 3.4 %copy.31 = f32[4,24,32,2,32]{2,0,4,1,3:T(4,128)} copy(f32[4,24,32,2,32]{4,3,2,1,0:T(2,128)S(1)} %reshape.66) | data formatting | bytes 1572864 | tf_op jit(solution)/shard_map/reshape | solution.py:272
  85.8 0.0 copy-start.1
  85.8 0.0 copy-start.6
  85.8 5.4 %reshape.67 = f32[48,4096]{1,0:T(8,128)} reshape(f32[2,24,32,4,32]{4,3,2,1,0:T(4,128)} %bitcast.59) | data formatting | bytes 1572864 | tf_op jit(solution)/shard_map/reshape | solution.py:275
  91.2 0.0 all-gather.5.cloned.1.call-update
  91.2 0.0 all-gather.7.cloned.1.call-start
  91.2 0.0 copy-done.1
  91.2 1.0 copy.34
  92.2 0.0 copy-done.6
  92.2 1.7 fusion.2
  93.9 0.9 reshape.68
  94.8 0.2 copy.45
  95.0 0.7 reshape.69
  95.7 4.2 %all_to_all.10 = f32[2,48,1024]{2,1,0:T(8,128)S(1)} all-to-all(f32[2,48,1024]{2,1,0:T(8,128)S(1)} %reshape.69), channel_id=1, replica_groups=mesh['grp'=2,'col'=4,'row'=2,'seq'=2] {'seq'}, dimensions={0} | all-to-all | bytes 786432 | tf_op jit(solution)/shard_map/all_to_all | solution.py:279
  99.9 0.2 copy.33
  100.1 0.8 pad_bitcast_fusion.right_ref
  101.0 0.0 all-gather.5.cloned.1.call-done
  101.0 2.9 %pad.18.left_ref = f32[128,4096]{1,0:T(8,128)} pad(f32[96,4096]{1,0:T(8,128)} %all-gather.5.cloned.1.call-done, f32[]{:T(128)} %constant.12.clone.1), padding=0_32x0_0 | pad | bytes 3670020 | tf_op jit(solution)/shard_map/jit(_pad)/pad | solution.py:281
  103.9 0.0 copy-start.2
  103.9 23.1 %shard_map.104 = (f32[4096,128]{1,0:T(8,128)}, f32[32,8,128]{2,1,0:T(8,128)}) custom-call(s32[1]{0:T(128)} %bitcast.part_ref, f32[128,4096]{1,0:T(8,128)} %pad.18.left_ref, f32[1024,128]{1,0:T(8,128)} %pad_bitcast_fusion.right_ref, f32[128,1024]{1,0:T(8,128)} %bitcast.66, f32[8,128]{1,0:T(8,128)} %bitcast.70, f32[8192,128]{1,0:T(8,128)} %bitcast.64), custom_call_target="tpu_custom_call" | custom-call | tf_op jit(solution)/shard_map/pallas_call | solution.py:284
  127.0 0.0 all-gather.7.cloned.1.call-update
  127.0 0.0 copy-done.2
  127.0 0.0 copy-start
  127.0 0.1 copy.39
  127.1 0.8 select_maximum_fusion.final_ref
  127.9 1.2 reshape.72
  129.1 0.0 copy-start.3
  129.2 0.0 copy-start.4
  129.2 0.1 broadcast_in_dim.2
  129.2 1.0 reshape.73
  130.3 3.7 %all-to-all-start.1 = ((f32[8,256,32]{1,2,0:T(8,128)}), f32[8,256,32]{1,2,0:T(8,128)S(1)}, u32[]{:S(2)}, u32[]{:S(2)}) async-start(f32[8,256,32]{1,2,0:T(8,128)} %reshape.73), calls=%async_computation.1 | async-start | bytes 524288 | tf_op jit(solution)/shard_map/all_to_all | solution.py:308
  134.0 0.0 copy-done
  134.0 0.1 slice_bitcast_fusion.1
  134.0 0.9 pad_maximum_fusion.1.raw_ref
  134.9 0.0 copy-done.3
  134.9 0.0 copy-done.4
  134.9 0.9 select_maximum_fusion.1
  135.8 7.9 %all-to-all-done.1 = f32[8,256,32]{1,2,0:T(8,128)S(1)} async-done(((f32[8,256,32]{1,2,0:T(8,128)}), f32[8,256,32]{1,2,0:T(8,128)S(1)}, u32[]{:S(2)}, u32[]{:S(2)}) %all-to-all-start.1) | async-done | bytes 262176 | tf_op jit(solution)/shard_map/all_to_all | solution.py:308
  143.7 0.1 copy.36
  143.9 0.1 fusion.6
  143.9 0.9 exponential_divide_fusion.weights_ref
  144.8 20.4 %shard_map.105 = f32[24,32,128]{2,1,0:T(8,128)} custom-call(f32[256,256]{1,0:T(8,128)} %exponential_divide_fusion.weights_ref, f32[8,24,32,128]{3,2,1,0:T(8,128)} %bitcast.62, f32[24,32,128]{2,1,0:T(8,128)} %pad_maximum_fusion.own_ref, f32[24,32,128]{2,1,0:T(8,128)} %pad_maximum_fusion.1.raw_ref, f32[128,512]{1,0:T(8,128)} %get-tuple-element.19.source_ref, ...), custom_call_target="tpu_custom_call" | custom-call | tf_op jit(solution)/shard_map/pallas_call | solution.py:314
  165.1 1.3 fusion.30
  166.5 0.9 maximum_bitcast_fusion
  167.4 0.0 all-gather.7.cloned.1.call-done
  167.4 4.8 %copy.47 = f32[128,64,128]{2,1,0:T(8,128)} copy(f32[128,64,128]{2,1,0:T(8,128)} %all-gather.7.cloned.1.call-done) | data formatting | bytes 8388608
  (4 shorter events, 0.1 us)
Async XLA Ops:
  7.2 68.7 %copy-start.5 = (f32[64,32]{0,1:T(8,128)S(1)}, f32[64,32]{0,1:T(8,128)}, u32[]{:S(2)}) copy-start(f32[64,32]{0,1:T(8,128)} %param.11) | copy-start | bytes 24580
  7.2 68.6 %all-gather.9.cloned.1.call-start = ((), (), s32[]{:S(2)}) async-start(), calls=%async_computation.4 | async-start | bytes 3538944 | tf_op jit(solution)/shard_map/all_gather | solution.py:268
  12.9 88.1 %all-gather.5.cloned.1.call-start = ((), (), s32[]{:S(2)}) async-start(), calls=%async_computation.2 | async-start | bytes 2359296 | tf_op jit(solution)/shard_map/all_gather | solution.py:278
  85.8 5.4 %copy-start.1 = (f32[1024,128]{1,0:T(8,128)S(1)}, f32[1024,128]{1,0:T(8,128)}, u32[]{:S(2)}) copy-start(f32[1024,128]{1,0:T(8,128)} %param.13) | copy-start | bytes 1572868
  85.8 6.4 %copy-start.6 = (f32[64,32]{0,1:T(8,128)S(1)}, f32[64,32]{0,1:T(8,128)}, u32[]{:S(2)}) copy-start(f32[64,32]{0,1:T(8,128)} %param.12) | copy-start | bytes 24580
  91.2 76.3 %all-gather.7.cloned.1.call-start = ((), (), s32[]{:S(2)}) async-start(), calls=%async_computation.3 | async-start | bytes 6291456 | tf_op jit(solution)/shard_map/all_gather | solution.py:302
  103.9 23.1 %copy-start.2 = (f32[256,64]{0,1:T(8,128)S(1)}, f32[256,64]{0,1:T(8,128)}, u32[]{:S(2)}) copy-start(f32[256,64]{0,1:T(8,128)} %param.17) | copy-start | bytes 196612
  127.0 6.9 %copy-start = (f32[48,1,32,64]{3,2,1,0:T(8,128)S(1)}, f32[48,1,32,64]{3,2,1,0:T(8,128)}, u32[]{:S(2)}) copy-start(f32[48,1,32,64]{3,2,1,0:T(8,128)} %param.9) | copy-start | bytes 1179652
  129.1 5.8 %copy-start.3 = (f32[64,256]{1,0:T(8,128)S(1)}, f32[64,256]{1,0:T(8,128)}, u32[]{:S(2)}) copy-start(f32[64,256]{1,0:T(8,128)} %param.16) | copy-start | bytes 196612
  129.2 5.8 %copy-start.4 = (f32[64,256]{1,0:T(8,128)S(1)}, f32[64,256]{1,0:T(8,128)}, u32[]{:S(2)}) copy-start(f32[64,256]{1,0:T(8,128)} %param.15) | copy-start | bytes 196612
  130.3 13.4 %all-to-all-start.1 = ((f32[8,256,32]{1,2,0:T(8,128)}), f32[8,256,32]{1,2,0:T(8,128)S(1)}, u32[]{:S(2)}, u32[]{:S(2)}) async-start(f32[8,256,32]{1,2,0:T(8,128)} %reshape.73), calls=%async_computation.1 | async-start | bytes 524288 | tf_op jit(solution)/shard_map/all_to_all | solution.py:308
Sparse Core Ops, SparseCore 0:
  13.0 62.7 all-gather.8
  91.3 8.6 all-gather.4
  127.1 13.6 all-gather.6

commit v2 on v0

--- a/solution.py
+++ b/solution.py
@@ -1,6 +1,10 @@
+import functools
+
 import jax
 import jax.numpy as jnp
 from jax import lax
+from jax.experimental import pallas as pl
+from jax.experimental.pallas import tpu as pltpu
 from jax.sharding import PartitionSpec as P
 
 epsilon = 1e-05
@@ -27,7 +31,7 @@
     )
 
 
-def on_device(
+def general_path(
     alignment_tensor,
     residue_couplings,
     first_factor_matrix,
@@ -110,6 +114,455 @@
     return (revised_alignment, revised_couplings)
 
 
+f32, bf16 = jnp.float32, jnp.bfloat16
+LANES = 128
+
+
+def halves(values):
+    high = values.astype(bf16)
+    return high, (values - high.astype(f32)).astype(bf16)
+
+
+def mm(a, b):
+    return jnp.dot(a, b, preferred_element_type=f32)
+
+
+def mm3(a, b):
+    (a_high, a_low), (b_high, b_low) = a, b
+    return mm(a_high, b_high) + (mm(a_high, b_low) + mm(a_low, b_high))
+
+
+def nt(a, b):
+    return lax.dot_general(a, b, (((1,), (1,)), ((), ())), preferred_element_type=f32)
+
+
+def nt3(a, b):
+    (a_high, a_low), (b_high, b_low) = a, b
+    return nt(a_high, b_high) + (nt(a_high, b_low) + nt(a_low, b_high))
+
+
+def block_kernel(
+    row_size,
+    col_size,
+    seq_size,
+    heads,
+    raw_ref,
+    pair_ref,
+    first_ref,
+    second_ref,
+    product_ref,
+    score_ref,
+    source_ref,
+    gate_ref,
+    final_ref,
+    out_ref,
+    revised_ref,
+    own_s,
+    partner_s,
+    left_s,
+    right_s,
+    high_s,
+    low_s,
+    score_s,
+    sent_s,
+    received_s,
+    weight_s,
+    gates_s,
+    mixed_s,
+    block_send,
+    block_recv,
+    partner_send,
+    partner_recv,
+    score_send,
+    score_recv,
+    pair_sem,
+):
+    seqs, own, depth = raw_ref.shape
+    groups = seqs // 2
+    rows, cols, channels = revised_ref.shape
+    outer = first_ref.shape[0] // 2
+    half_cols = cols // seq_size
+    total = seqs * seq_size
+    wide = source_ref.shape[1]
+    entries = heads * own
+    members = col_size * seq_size
+    row, col, seq = (lax.axis_index(a) for a in ("row", "col", "seq"))
+    other_row, other_seq = 1 - row, 1 - seq
+    me = col * seq_size + seq
+    mine = row * col_size + col
+
+    def normalize(step, carry):
+        parts = []
+        for t in range(2):
+            part = standardize_entries(raw_ref[step + t * groups])
+            parts.append(part)
+        at = pl.ds(pl.multiple_of(step * own, own), own)
+        own_s[mine, at, :] = jnp.concatenate(parts, axis=-1)
+        return carry
+
+    lax.fori_loop(0, groups, normalize, 0, unroll=4)
+
+    barrier = pltpu.get_barrier_semaphore()
+
+    def member(offset):
+        other = lax.rem(me + offset, members)
+        return {"col": other // seq_size, "seq": lax.rem(other, seq_size)}
+
+    for offset in range(1, members):
+        pl.semaphore_signal(barrier, inc=1, device_id=member(offset), device_id_type=pl.DeviceIdType.MESH)
+    pl.semaphore_signal(barrier, inc=1, device_id={"row": other_row}, device_id_type=pl.DeviceIdType.MESH)
+    pl.semaphore_wait(barrier, members)
+
+    started = []
+
+    def ship(slot, target, send, condition, to=None, sems=None):
+        copy = pltpu.make_async_remote_copy(
+            src_ref=own_s.at[slot],
+            dst_ref=(own_s if to is None else to).at[slot],
+            send_sem=send,
+            recv_sem=(block_recv if sems is None else sems).at[slot],
+            device_id=target,
+            device_id_type=pl.DeviceIdType.MESH,
+        )
+        started.append((copy, condition))
+        run(condition, copy.start)
+
+    def run(condition, action):
+        if condition is None:
+            action()
+        else:
+            pl.when(condition)(action)
+
+    def both(a, b):
+        return b if a is None else (a if b is None else jnp.logical_and(a, b))
+
+    def arrived(buffer, sems, slot):
+        return pltpu.make_async_remote_copy(
+            src_ref=buffer.at[slot],
+            dst_ref=buffer.at[slot],
+            send_sem=block_send.at[0],
+            recv_sem=sems.at[slot],
+            device_id={"row": other_row},
+            device_id_type=pl.DeviceIdType.MESH,
+        ).wait_recv
+
+    counter = [0]
+
+    def next_send():
+        counter[0] += 1
+        return block_send.at[counter[0] - 1]
+
+    def relay(slot, rightward, leftward, exists):
+        if rightward:
+            ship(slot, {"col": col + 1}, next_send(), both(exists, col < col_size - 1))
+        if leftward:
+            ship(slot, {"col": col - 1}, next_send(), both(exists, col > 0))
+        ship(slot, {"row": other_row}, next_send(), exists)
+        ship(slot, {"seq": other_seq}, next_send(), exists, partner_s, partner_recv)
+
+    relay(mine, True, True, None)
+    for step in range(1, col_size):
+        from_left = jnp.logical_and(col >= step, True)
+        run(from_left, arrived(own_s, block_recv, mine - step))
+        relay(mine - step, True, False, from_left)
+        from_right = jnp.logical_and(col + step < col_size, True)
+        run(from_right, arrived(own_s, block_recv, mine + step))
+        relay(mine + step, False, True, from_right)
+
+    column_row = (col * seq_size) // col_size
+    column_at = lax.rem(col * seq_size, col_size)
+    elsewhere = column_row != row
+    here = jnp.logical_not(elsewhere)
+    needed = other_row * col_size + column_at
+    for t in range(seq_size):
+        run(elsewhere, arrived(own_s, block_recv, needed + t))
+    ship(
+        other_row * col_size + column_at + other_seq,
+        {"seq": other_seq},
+        next_send(),
+        elsewhere,
+        partner_s,
+        partner_recv,
+    )
+    for block in range(col_size):
+        arrived(partner_s, partner_recv, row * col_size + block)()
+    run(elsewhere, arrived(partner_s, partner_recv, needed + seq))
+
+    first = halves(first_ref[...])
+    second = halves(second_ref[...])
+    first_slot = row * col_size
+
+    def project_left(group, carry):
+        at = pl.ds(pl.multiple_of(group * own, own), own)
+        for source, buffer in enumerate((own_s, partner_s)):
+            tokens = buffer[pl.ds(first_slot, col_size), at, :].reshape(rows, LANES)
+            result = nt3(first, halves(tokens))
+            for half in range(2):
+                place = half * seqs + source * groups + group
+                left_s[pl.ds(pl.multiple_of(place * outer, outer), outer), :] = result[
+                    half * outer : (half + 1) * outer
+                ]
+        return carry
+
+    lax.fori_loop(0, groups, project_left, 0, unroll=4)
+    column_slot = col * seq_size + seq
+    room = jnp.zeros((outer, LANES - total), f32)
+
+    def project_right(token, carry):
+        tokens = jnp.concatenate(
+            [buffer[column_slot, pl.ds(token, groups, stride=own), :] for buffer in (own_s, partner_s)], axis=0
+        )
+        result = nt3(second, halves(tokens))
+        placed = jnp.concatenate([result[:outer], result[outer:], room], axis=1)
+        right_s[pl.ds(pl.multiple_of(token * outer, outer), outer), :] = placed
+        return carry
+
+    lax.fori_loop(0, half_cols, project_right, 0, unroll=4)
+
+    r_high, r_low = halves(right_s[...])
+    r_both = jnp.concatenate([r_high, r_low], axis=1)
+    blank = jnp.zeros((LANES - total, 2 * rows), f32)
+
+    def outer_step(step, carry):
+        pieces = [left_s[pl.ds(2 * step + t, total, stride=outer), :] for t in range(2)]
+        l_high, l_low = halves(jnp.concatenate([jnp.concatenate(pieces, axis=1), blank], axis=0))
+        product = mm(r_both, jnp.concatenate([l_high, l_high], axis=0)) + mm(r_high, l_low)
+        p_high, p_low = halves(product)
+        for t in range(2):
+            high_s[2 * step + t] = p_high[:, t * rows : (t + 1) * rows]
+            low_s[2 * step + t] = p_low[:, t * rows : (t + 1) * rows]
+        return carry
+
+    lax.fori_loop(0, outer // 2, outer_step, 0)
+    t_high, t_low = halves(product_ref[...])
+    t_both = jnp.concatenate([t_high, t_low], axis=0)
+    c_halves = halves(score_ref[...])
+    first_col = seq * half_cols
+    flat_pair = pair_ref.reshape(rows * cols, channels)
+    flat_revised = revised_ref.reshape(rows * cols, channels)
+
+    def pair_step(step, carry):
+        def block(ref):
+            pieces = [
+                ref[:, pl.ds(pl.multiple_of((2 * step + t) * outer, outer), outer), :].reshape(outer * outer, rows)
+                for t in range(2)
+            ]
+            return jnp.concatenate(pieces, axis=1)
+
+        joint = mm(t_both, block(high_s))
+        update = (joint[:channels] + (joint[channels:] + mm(t_high, block(low_s)))) / total
+        for t in range(2):
+            column = 2 * step + t
+            at = pl.ds(first_col + column, rows, stride=cols)
+            revised = flat_pair[at, :].T + update[:, t * rows : (t + 1) * rows]
+            flat_revised[at, :] = revised.T
+            center = revised - jnp.mean(revised, axis=0, keepdims=True)
+            spread = jnp.mean(center * center, axis=0, keepdims=True)
+            score_s[column] = mm3(c_halves, halves(center / jnp.sqrt(spread + epsilon)))
+        return carry
+
+    lax.fori_loop(0, half_cols // 2, pair_step, 0)
+
+    pack_count = LANES // own
+    quarter = half_cols // pack_count
+    scores = score_s[...].reshape(pack_count, quarter, heads, rows)
+    for block in range(col_size):
+        cut = [scores[t, :, :, block * own : (block + 1) * own] for t in range(pack_count)]
+        sent_s[block] = jnp.concatenate(cut, axis=-1)
+    received_s[me] = sent_s[col]
+    own_rows = halves(own_s[mine])
+    gates_s[...] = jax.nn.sigmoid(mm3(own_rows, halves(gate_ref[...]))).reshape(groups, own, wide)
+    score_copies = []
+    for offset in range(1, members):
+        target = member(offset)
+        copy = pltpu.make_async_remote_copy(
+            src_ref=sent_s.at[target["col"]],
+            dst_ref=received_s.at[me],
+            send_sem=score_send.at[offset],
+            recv_sem=score_recv.at[me],
+            device_id=target,
+            device_id_type=pl.DeviceIdType.MESH,
+        )
+        copy.start()
+        score_copies.append(copy)
+    half_pair = revised_ref.at[:, pl.ds(pl.multiple_of(first_col, half_cols), half_cols), :]
+    pair_copy = pltpu.make_async_remote_copy(
+        src_ref=half_pair,
+        dst_ref=half_pair,
+        send_sem=pair_sem.at[0],
+        recv_sem=pair_sem.at[1],
+        device_id={"seq": other_seq},
+        device_id_type=pl.DeviceIdType.MESH,
+    )
+    pair_copy.start()
+    for offset in range(1, members):
+        arrived(received_s, score_recv, lax.rem(me + offset, members))()
+    for t in range(seq_size):
+        run(here, arrived(own_s, block_recv, other_row * col_size + column_at + t))
+    last_at = lax.rem(column_at + seq_size, col_size)
+    for t in range(col_size - seq_size):
+        arrived(own_s, block_recv, other_row * col_size + last_at + t)()
+
+    logits = received_s[...].reshape(members * quarter, heads, LANES)
+
+    def over_lanes(values, op):
+        result = values
+        for t in range(1, pack_count):
+            result = op(result, pltpu.roll(values, t * own, 1))
+        return result
+
+    top = over_lanes(jnp.max(logits, axis=0), jnp.maximum)
+    powers = jnp.exp(logits - top[None])
+    weights = powers / over_lanes(jnp.sum(powers, axis=0), jnp.add)[None]
+    weight_s[...] = weights.reshape(members * quarter * heads, LANES)
+    lines = []
+    for head in range(heads):
+        turned = weight_s[pl.ds(head, members * quarter, stride=heads), :].T
+        lines.append(jnp.concatenate([turned[t * own : (t + 1) * own] for t in range(pack_count)], axis=1))
+    w_high, w_low = halves(jnp.concatenate(lines, axis=0))
+    w_both = jnp.concatenate([w_high, w_low], axis=0)
+    s_high, s_low = halves(source_ref[...])
+    s_twice = jnp.concatenate([s_high, s_high], axis=0)
+    row_head = lax.broadcasted_iota(jnp.int32, (entries, wide), 0) // own
+    lane_head = lax.broadcasted_iota(jnp.int32, (entries, wide), 1) // (wide // 2 // heads) % heads
+    mask = row_head == lane_head
+
+    def mix_step(group, carry):
+        pieces = [
+            own_s[:, pl.ds(pl.multiple_of(group * own + t * quarter, quarter), quarter), :].reshape(-1, LANES)
+            for t in range(pack_count)
+        ]
+        x_high, x_low = halves(jnp.concatenate(pieces, axis=0))
+        values = mm(jnp.concatenate([x_high, x_low], axis=1), s_twice) + mm(x_high, s_low)
+        v_high, v_low = halves(values)
+        joint = mm(w_both, v_high)
+        full = joint[:entries] + (joint[entries:] + mm(w_high, v_low))
+        mixed = jnp.sum(jnp.where(mask, full, 0.0).reshape(heads, own, wide), axis=0)
+        mixed_s[group] = mixed * gates_s[group]
+        return carry
+
+    lax.fori_loop(0, groups, mix_step, 0)
+    result = mm3(halves(mixed_s[...].reshape(groups * own, wide)), halves(final_ref[...]))
+    result = result.reshape(groups, own, LANES)
+    for t in range(2):
+        at = pl.ds(t * groups, groups)
+        out_ref[at] = raw_ref[at] + result[:, :, t * depth : (t + 1) * depth]
+
+    for copy, condition in started:
+        run(condition, copy.wait_send)
+    for copy in score_copies:
+        copy.wait_send()
+    pair_copy.wait_send()
+    other_half = revised_ref.at[:, pl.ds(pl.multiple_of(other_seq * half_cols, half_cols), half_cols), :]
+    pltpu.make_async_remote_copy(
+        src_ref=other_half,
+        dst_ref=other_half,
+        send_sem=pair_sem.at[0],
+        recv_sem=pair_sem.at[1],
+        device_id={"seq": other_seq},
+        device_id_type=pl.DeviceIdType.MESH,
+    ).wait_recv()
+
+
+def twice(matrix):
+    zero = jnp.zeros_like(matrix)
+    return jnp.concatenate(
+        [jnp.concatenate([matrix, zero], axis=1), jnp.concatenate([zero, matrix], axis=1)], axis=0
+    )
+
+
+def fast_path(
+    alignment_tensor,
+    residue_couplings,
+    first_factor_matrix,
+    second_factor_matrix,
+    tensor_product_matrix,
+    coupling_score_matrix,
+    averaged_source_matrix,
+    sigmoid_matrix,
+    final_matrix,
+):
+    seqs, _, own, depth = alignment_tensor.shape
+    rows, cols, channels = residue_couplings.shape
+    outer = first_factor_matrix.shape[1]
+    heads = coupling_score_matrix.shape[1]
+    row_size, col_size, seq_size = (lax.axis_size(a) for a in ("row", "col", "seq"))
+    total = seqs * seq_size
+    blocks = row_size * col_size
+    half_cols = cols // seq_size
+    members = col_size * seq_size
+    groups = seqs // 2
+    wide = 2 * averaged_source_matrix.shape[1]
+    quarter = half_cols * own // LANES
+    vmem = pl.BlockSpec(memory_space=pltpu.VMEM)
+    dma = pltpu.SemaphoreType.DMA
+    revised_alignment, revised_couplings = pl.pallas_call(
+        functools.partial(block_kernel, row_size, col_size, seq_size, heads),
+        out_shape=(
+            jax.ShapeDtypeStruct((seqs, own, depth), f32),
+            jax.ShapeDtypeStruct((rows, cols, channels), f32),
+        ),
+        in_specs=[vmem] * 9,
+        out_specs=(vmem, vmem),
+        scratch_shapes=[
+            pltpu.VMEM((blocks, groups * own, LANES), f32),
+            pltpu.VMEM((blocks, groups * own, LANES), f32),
+            pltpu.VMEM((total * outer, rows), f32),
+            pltpu.VMEM((half_cols * outer, LANES), f32),
+            pltpu.VMEM((outer, half_cols * outer, rows), bf16),
+            pltpu.VMEM((outer, half_cols * outer, rows), bf16),
+            pltpu.VMEM((half_cols, heads, rows), f32),
+            pltpu.VMEM((col_size, quarter, heads, LANES), f32),
+            pltpu.VMEM((members, quarter, heads, LANES), f32),
+            pltpu.VMEM((members * quarter * heads, LANES), f32),
+            pltpu.VMEM((groups, own, wide), f32),
+            pltpu.VMEM((groups, own, wide), f32),
+            dma((32,)),
+            dma((blocks,)),
+            dma((1,)),
+            dma((blocks,)),
+            dma((members,)),
+            dma((members,)),
+            dma((2,)),
+        ],
+        compiler_params=pltpu.CompilerParams(
+            collective_id=0, has_side_effects=True, vmem_limit_bytes=60 << 20
+        ),
+    )(
+        alignment_tensor.reshape(seqs, own, depth),
+        residue_couplings,
+        twice(first_factor_matrix).T,
+        twice(second_factor_matrix).T,
+        tensor_product_matrix.T,
+        coupling_score_matrix.T,
+        twice(averaged_source_matrix),
+        twice(sigmoid_matrix),
+        twice(final_matrix),
+    )
+    return revised_alignment.reshape(alignment_tensor.shape), revised_couplings
+
+
+def on_device(alignment_tensor, residue_couplings, first_factor_matrix, *rest):
+    seqs, tiles, own, depth = alignment_tensor.shape
+    rows, cols, channels = residue_couplings.shape
+    row_size, col_size, seq_size = (lax.axis_size(a) for a in ("row", "col", "seq"))
+    fits = (
+        tiles == 1
+        and rows == own * col_size == LANES
+        and cols == own * seq_size
+        and row_size * rows == col_size * cols
+        and own % 16 == 0
+        and seqs % 6 == 0
+        and 2 * depth == channels == LANES
+        and first_factor_matrix.shape[1] % 16 == 0
+        and seq_size == row_size == 2
+        and rest[2].shape[1] == 8 == own * own // LANES
+        and seqs * seq_size <= LANES
+    )
+    path = fast_path if fits else general_path
+    return path(alignment_tensor, residue_couplings, first_factor_matrix, *rest)
+
+
 def solution(mesh):
     return jax.shard_map(
         on_device,

time: 620 us -> 112 us (0.18); the launches traced: 612 us -> 112 us
  waiting for transfers between devices: 231 us -> 0 us
  matrix products: 221 us -> 0 us
  Pallas kernels: 0 us -> 97.2 us
  local copies, waits for them, and re-layouts: 74.5 us -> 9.82 us
  blocking collectives: 36.6 us -> 0 us
  loops' own time: 15.9 us -> 0 us
  other arithmetic: 18.9 us -> 4.12 us
  between operations: 14.3 us -> 0.64 us
    dot_general x22 -> x0, matrix products: 221 us -> none  [the longest x8 113 us: outer_block(): jnp.dot(flat_prod, tensor_product_matrix, precision=exact_arithmetic)]
    reduce_scatter x1 -> x0, waiting for transfers between devices: 107 us -> none  [on_device(): lax.psum_scatter(mixed_rows, 'col', scatter_dimension=1, tiled=True)]
    pallas_call x0 -> x1, Pallas kernels: none -> 97.2 us  [fast_path(): pl.pallas_call(functools.partial(block_kernel, row_size, col_size, seq_si...]
    all_gather x1 -> x0, waiting for transfers between devices: 67 us -> none  [on_device(): gathered_lines = lax.all_gather(alignment_tensor, 'col', axis=2, tiled=True)]
    psum x2 -> x0, waiting for transfers between devices: 56 us -> none  [the longest x1 35.1 us: broadcast(): return lax.psum(block, axis)]
    div x9 -> x0, local copies, waits for them, and re-layouts: 52 us -> none  [the longest x8 51.9 us: outer_block(): jnp.einsum('sic,sje->ijce', left_block, second_factor_tile, precision=exa...]
    pmax x1 -> x0, blocking collectives: 19.9 us -> none  [on_device(): score_top = lax.pmax(local_top, 'col')]
    psum x1 -> x0, blocking collectives: 16.7 us -> none  [on_device(): lax.psum(jnp.sum(jnp.exp(scores - score_top[:, :, None]), axis=2), 'col')]
  transfers between devices with their start and end apart: 4 -> 0, of which waited for: 4 -> 0; matrix products, arithmetic and copies ran while one was open for 4% -> 0% of each run, Pallas kernels for 0% -> 0%
where the time goes in v2:
time: 112 us
  Pallas kernels  97.2 us (87%)
  local copies, waits for them, and re-layouts  9.82 us (9%)
  other arithmetic  4.12 us (4%)
    pallas_call x1, Pallas kernels, fast_path(): pl.pallas_call(functools.partial(block_kernel, row_size, col_size, seq_si...  97.2 us
    unnamed x4, local copies, waits for them, and re-layouts  9.82 us
    concatenate x2, other arithmetic, twice(): jnp.concatenate([jnp.concatenate([matrix, zero], axis=1), jnp.concatenate...  2.59 us

profile of v2, /device:TPU:0, one launch (start us, length us, event | category | flops | bytes accessed | tf_op | source)
XLA Modules:
  0.0 111.8 jit_solution(756834000723093129)
XLA Ops:
  0.6 1.5 %fusion = (f32[64,128]{1,0:T(8,128)}, f32[64,128]{1,0:T(8,128)}) fusion(f32[64,32]{0,1:T(8,128)} %param.12, f32[64,32]{0,1:T(8,128)} %param.11), kind=kLoop, calls=%fused_computation.8 | loop fusion | flops 65536 | bytes 81920 | tf_op jit(solution)/shard_map/transpose | solution.py:535
  2.2 0.9 copy.12
  3.1 0.8 select_maximum_fusion.final_ref
  3.9 2.0 %copy.11 = f32[1024,128]{0,1:T(8,128)} copy(f32[1024,128]{1,0:T(8,128)} %param.13) | data formatting | bytes 1048576 | tf_op args[4]
  5.9 1.8 %select_maximum_fusion.1 = (f32[128,512]{1,0:T(8,128)}, f32[128,512]{1,0:T(8,128)}) fusion(f32[64,256]{1,0:T(8,128)} %param.16, f32[64,256]{1,0:T(8,128)} %param.15), kind=kLoop, calls=%fused_computation.3 | loop fusion | flops 524288 | bytes 655360 | tf_op jit(solution)/shard_map/concatenate | solution.py:469
  7.7 97.2 %shard_map.104 = (f32[48,32,64]{2,1,0:T(8,128)}, f32[128,64,128]{2,1,0:T(8,128)}) custom-call(f32[48,32,64]{2,1,0:T(8,128)} %bitcast.12, f32[128,64,128]{2,1,0:T(8,128)} %pair_ref.1, f32[64,128]{1,0:T(8,128)} %get-tuple-element.11.first_ref, f32[64,128]{1,0:T(8,128)} %get-tuple-element.10.second_ref, f32[128,1024]{1,0:T(8,128)} %bitcast.10, ...), custom_call_target="tpu_custom_call" | custom-call | tf_op jit(solution)/shard_map/pallas_call | solution.py:499
  104.9 2.1 %copy.17 = f32[48,1,32,64]{3,2,1,0:T(8,128)} copy(f32[48,1,32,64]{3,2,1,0:T(8,128)} %bitcast.11) | data formatting | bytes 786432
  107.0 4.8 %copy.18 = f32[128,64,128]{2,1,0:T(8,128)} copy(f32[128,64,128]{2,1,0:T(8,128)} %get-tuple-element.15) | data formatting | bytes 8388608

commit v3 on v2

--- a/solution.py
+++ b/solution.py
@@ -158,7 +158,9 @@
     out_ref,
     revised_ref,
     own_s,
-    partner_s,
+    l_s,
+    r_own,
+    r_s,
     left_s,
     right_s,
     high_s,
@@ -171,8 +173,9 @@
     mixed_s,
     block_send,
     block_recv,
-    partner_send,
-    partner_recv,
+    l_recv,
+    r_recv,
+    local_sem,
     score_send,
     score_recv,
     pair_sem,
@@ -202,6 +205,36 @@
 
     lax.fori_loop(0, groups, normalize, 0, unroll=4)
 
+    first = halves(first_ref[...])
+    second = halves(second_ref[...])
+    pairs = LANES // 2 // own
+    left_steps = groups // pairs
+
+    def project_left(step, carry):
+        parts = []
+        for t in range(pairs):
+            at = pl.ds(pl.multiple_of((t * left_steps + step) * own, own), own)
+            result = nt3(first, halves(own_s[mine, at, :]))
+            parts += [result[:outer], result[outer:]]
+        l_s[col, seq, pl.ds(pl.multiple_of(step * outer, outer), outer), :] = jnp.concatenate(parts, axis=1)
+        return carry
+
+    lax.fori_loop(0, left_steps, project_left, 0, unroll=4)
+    span = LANES // 2
+    room = jnp.zeros((outer, span - seqs), f32)
+    right_steps = half_cols // 2
+
+    def project_right(step, carry):
+        parts = []
+        for t in range(2):
+            tokens = own_s[mine, pl.ds(t * right_steps + step, groups, stride=own), :]
+            result = nt3(second, halves(tokens))
+            parts += [result[:outer], result[outer:], room]
+        r_own[pl.ds(pl.multiple_of(step * outer, outer), outer), :] = jnp.concatenate(parts, axis=1)
+        return carry
+
+    lax.fori_loop(0, right_steps, project_right, 0, unroll=4)
+
     barrier = pltpu.get_barrier_semaphore()
 
     def member(offset):
@@ -215,12 +248,12 @@
 
     started = []
 
-    def ship(slot, target, send, condition, to=None, sems=None):
+    def ship(source, place, target, sem, condition):
         copy = pltpu.make_async_remote_copy(
-            src_ref=own_s.at[slot],
-            dst_ref=(own_s if to is None else to).at[slot],
-            send_sem=send,
-            recv_sem=(block_recv if sems is None else sems).at[slot],
+            src_ref=source,
+            dst_ref=place,
+            send_sem=next_send(),
+            recv_sem=sem,
             device_id=target,
             device_id_type=pl.DeviceIdType.MESH,
         )
@@ -236,12 +269,12 @@
     def both(a, b):
         return b if a is None else (a if b is None else jnp.logical_and(a, b))
 
-    def arrived(buffer, sems, slot):
+    def arrived(place, sem):
         return pltpu.make_async_remote_copy(
-            src_ref=buffer.at[slot],
-            dst_ref=buffer.at[slot],
+            src_ref=place,
+            dst_ref=place,
             send_sem=block_send.at[0],
-            recv_sem=sems.at[slot],
+            recv_sem=sem,
             device_id={"row": other_row},
             device_id_type=pl.DeviceIdType.MESH,
         ).wait_recv
@@ -252,80 +285,92 @@
         counter[0] += 1
         return block_send.at[counter[0] - 1]
 
-    def relay(slot, rightward, leftward, exists):
+    def relay_left(at, rightward, leftward, exists):
+        place, sem = l_s.at[at, seq], l_recv.at[at, seq]
         if rightward:
-            ship(slot, {"col": col + 1}, next_send(), both(exists, col < col_size - 1))
+            ship(place, place, {"col": col + 1}, sem, both(exists, col < col_size - 1))
         if leftward:
-            ship(slot, {"col": col - 1}, next_send(), both(exists, col > 0))
-        ship(slot, {"row": other_row}, next_send(), exists)
-        ship(slot, {"seq": other_seq}, next_send(), exists, partner_s, partner_recv)
-
-    relay(mine, True, True, None)
+            ship(place, place, {"col": col - 1}, sem, both(exists, col > 0))
+        ship(place, place, {"seq": other_seq}, sem, exists)
+
+    def relay(slot, rightward, leftward, across, exists):
+        place, sem = own_s.at[slot], block_recv.at[slot]
+        if rightward:
+            ship(place, place, {"col": col + 1}, sem, both(exists, col < col_size - 1))
+        if leftward:
+            ship(place, place, {"col": col - 1}, sem, both(exists, col > 0))
+        if across:
+            ship(place, place, {"row": other_row}, sem, exists)
+
+    def relay_step(step):
+        run(col >= step, arrived(own_s.at[mine - step], block_recv.at[mine - step]))
+        relay(mine - step, True, False, True, col >= step)
+        run(col + step < col_size, arrived(own_s.at[mine + step], block_recv.at[mine + step]))
+        relay(mine + step, False, True, True, col + step < col_size)
+
+    relay_left(col, True, True, None)
+    column_slot = col * seq_size + seq
+    here = column_slot // col_size == row
+    elsewhere = jnp.logical_not(here)
+    target_col, target_seq = mine // seq_size, lax.rem(mine, seq_size)
+    own_right = jnp.logical_and(target_col == col, target_seq == seq)
+    ship(
+        r_own, r_s.at[seq], {"col": target_col, "seq": target_seq}, r_recv.at[seq], jnp.logical_not(own_right)
+    )
+    ship(own_s.at[mine], own_s.at[mine], {"row": other_row}, block_recv.at[mine], elsewhere)
+
+    @pl.when(own_right)
+    def _():
+        keep = pltpu.make_async_copy(r_own, r_s.at[seq], local_sem.at[0])
+        keep.start()
+        keep.wait()
+
     for step in range(1, col_size):
-        from_left = jnp.logical_and(col >= step, True)
-        run(from_left, arrived(own_s, block_recv, mine - step))
-        relay(mine - step, True, False, from_left)
-        from_right = jnp.logical_and(col + step < col_size, True)
-        run(from_right, arrived(own_s, block_recv, mine + step))
-        relay(mine + step, False, True, from_right)
-
-    column_row = (col * seq_size) // col_size
-    column_at = lax.rem(col * seq_size, col_size)
-    elsewhere = column_row != row
-    here = jnp.logical_not(elsewhere)
-    needed = other_row * col_size + column_at
-    for t in range(seq_size):
-        run(elsewhere, arrived(own_s, block_recv, needed + t))
-    ship(
-        other_row * col_size + column_at + other_seq,
-        {"seq": other_seq},
-        next_send(),
-        elsewhere,
-        partner_s,
-        partner_recv,
-    )
-    for block in range(col_size):
-        arrived(partner_s, partner_recv, row * col_size + block)()
-    run(elsewhere, arrived(partner_s, partner_recv, needed + seq))
-
-    first = halves(first_ref[...])
-    second = halves(second_ref[...])
-    first_slot = row * col_size
-
-    def project_left(group, carry):
-        at = pl.ds(pl.multiple_of(group * own, own), own)
-        for source, buffer in enumerate((own_s, partner_s)):
-            tokens = buffer[pl.ds(first_slot, col_size), at, :].reshape(rows, LANES)
-            result = nt3(first, halves(tokens))
-            for half in range(2):
-                place = half * seqs + source * groups + group
-                left_s[pl.ds(pl.multiple_of(place * outer, outer), outer), :] = result[
-                    half * outer : (half + 1) * outer
-                ]
+        run(col >= step, arrived(l_s.at[col - step, seq], l_recv.at[col - step, seq]))
+        relay_left(col - step, True, False, col >= step)
+        run(col + step < col_size, arrived(l_s.at[col + step, seq], l_recv.at[col + step, seq]))
+        relay_left(col + step, False, True, col + step < col_size)
+        if step == 1:
+            source_here = lax.rem(column_slot, col_size) == col
+            for source in range(seq_size):
+                kept = jnp.logical_and(source_here, seq == source)
+                run(jnp.logical_and(here, jnp.logical_not(kept)), arrived(r_s.at[source], r_recv.at[source]))
+                ship(r_s.at[source], r_s.at[source], {"row": other_row}, r_recv.at[source], here)
+            ship(own_s.at[mine], own_s.at[mine], {"row": other_row}, block_recv.at[mine], here)
+    relay(mine, True, True, False, None)
+    for source in range(seq_size):
+        run(elsewhere, arrived(r_s.at[source], r_recv.at[source]))
+    for at in range(col_size):
+        arrived(l_s.at[at, other_seq], l_recv.at[at, other_seq])()
+
+    blank = jnp.zeros(((span - seqs) * outer, rows), f32)
+    for source in range(seq_size):
+        left_s[(source * span + seqs) * outer : (source + 1) * span * outer, :] = blank
+
+    def place_left(step, carry):
+        at = pl.ds(pl.multiple_of(step * outer, outer), outer)
+        for source in range(seq_size):
+            blocks = [l_s[t, source, at, :] for t in range(col_size)]
+            for t in range(pairs):
+                for half in range(2):
+                    lane = (2 * t + half) * own
+                    line = jnp.concatenate([block[:, lane : lane + own] for block in blocks], axis=1)
+                    place = source * span + half * groups + t * left_steps + step
+                    left_s[pl.ds(pl.multiple_of(place * outer, outer), outer), :] = line
         return carry
 
-    lax.fori_loop(0, groups, project_left, 0, unroll=4)
-    column_slot = col * seq_size + seq
-    room = jnp.zeros((outer, LANES - total), f32)
-
-    def project_right(token, carry):
-        tokens = jnp.concatenate(
-            [buffer[column_slot, pl.ds(token, groups, stride=own), :] for buffer in (own_s, partner_s)], axis=0
+    lax.fori_loop(0, left_steps, place_left, 0, unroll=2)
+    for t in range(2):
+        right_s[t * right_steps * outer : (t + 1) * right_steps * outer, :] = jnp.concatenate(
+            [r_s[source, :, t * span : (t + 1) * span] for source in range(seq_size)], axis=1
         )
-        result = nt3(second, halves(tokens))
-        placed = jnp.concatenate([result[:outer], result[outer:], room], axis=1)
-        right_s[pl.ds(pl.multiple_of(token * outer, outer), outer), :] = placed
-        return carry
-
-    lax.fori_loop(0, half_cols, project_right, 0, unroll=4)
 
     r_high, r_low = halves(right_s[...])
     r_both = jnp.concatenate([r_high, r_low], axis=1)
-    blank = jnp.zeros((LANES - total, 2 * rows), f32)
 
     def outer_step(step, carry):
-        pieces = [left_s[pl.ds(2 * step + t, total, stride=outer), :] for t in range(2)]
-        l_high, l_low = halves(jnp.concatenate([jnp.concatenate(pieces, axis=1), blank], axis=0))
+        pieces = [left_s[pl.ds(2 * step + t, LANES, stride=outer), :] for t in range(2)]
+        l_high, l_low = halves(jnp.concatenate(pieces, axis=1))
         product = mm(r_both, jnp.concatenate([l_high, l_high], axis=0)) + mm(r_high, l_low)
         p_high, p_low = halves(product)
         for t in range(2):
@@ -334,6 +379,7 @@
         return carry
 
     lax.fori_loop(0, outer // 2, outer_step, 0)
+    relay_step(1)
     t_high, t_low = halves(product_ref[...])
     t_both = jnp.concatenate([t_high, t_low], axis=0)
     c_halves = halves(score_ref[...])
@@ -361,7 +407,11 @@
             score_s[column] = mm3(c_halves, halves(center / jnp.sqrt(spread + epsilon)))
         return carry
 
-    lax.fori_loop(0, half_cols // 2, pair_step, 0)
+    bounds = [half_cols // 2 * t // (col_size - 1) for t in range(1, col_size)]
+    lax.fori_loop(0, bounds[-2], pair_step, 0)
+    for step in range(2, col_size - 1):
+        relay_step(step)
+    lax.fori_loop(bounds[-2], bounds[-1], pair_step, 0)
 
     pack_count = LANES // own
     quarter = half_cols // pack_count
@@ -385,6 +435,8 @@
         )
         copy.start()
         score_copies.append(copy)
+    if col_size > 2:
+        relay_step(col_size - 1)
     half_pair = revised_ref.at[:, pl.ds(pl.multiple_of(first_col, half_cols), half_cols), :]
     pair_copy = pltpu.make_async_remote_copy(
         src_ref=half_pair,
@@ -396,13 +448,8 @@
     )
     pair_copy.start()
     for offset in range(1, members):
-        arrived(received_s, score_recv, lax.rem(me + offset, members))()
-    for t in range(seq_size):
-        run(here, arrived(own_s, block_recv, other_row * col_size + column_at + t))
-    last_at = lax.rem(column_at + seq_size, col_size)
-    for t in range(col_size - seq_size):
-        arrived(own_s, block_recv, other_row * col_size + last_at + t)()
-
+        other = lax.rem(me + offset, members)
+        arrived(received_s.at[other], score_recv.at[other])()
     logits = received_s[...].reshape(members * quarter, heads, LANES)
 
     def over_lanes(values, op):
@@ -426,6 +473,9 @@
     row_head = lax.broadcasted_iota(jnp.int32, (entries, wide), 0) // own
     lane_head = lax.broadcasted_iota(jnp.int32, (entries, wide), 1) // (wide // 2 // heads) % heads
     mask = row_head == lane_head
+
+    for at in range(col_size):
+        arrived(own_s.at[other_row * col_size + at], block_recv.at[other_row * col_size + at])()
 
     def mix_step(group, carry):
         pieces = [
@@ -506,8 +556,10 @@
         out_specs=(vmem, vmem),
         scratch_shapes=[
             pltpu.VMEM((blocks, groups * own, LANES), f32),
-            pltpu.VMEM((blocks, groups * own, LANES), f32),
-            pltpu.VMEM((total * outer, rows), f32),
+            pltpu.VMEM((col_size, seq_size, groups // (LANES // 2 // own) * outer, LANES), f32),
+            pltpu.VMEM((half_cols // 2 * outer, LANES), f32),
+            pltpu.VMEM((seq_size, half_cols // 2 * outer, LANES), f32),
+            pltpu.VMEM((LANES * outer, rows), f32),
             pltpu.VMEM((half_cols * outer, LANES), f32),
             pltpu.VMEM((outer, half_cols * outer, rows), bf16),
             pltpu.VMEM((outer, half_cols * outer, rows), bf16),
@@ -517,10 +569,11 @@
             pltpu.VMEM((members * quarter * heads, LANES), f32),
             pltpu.VMEM((groups, own, wide), f32),
             pltpu.VMEM((groups, own, wide), f32),
-            dma((32,)),
+            dma((64,)),
             dma((blocks,)),
+            dma((col_size, seq_size)),
+            dma((seq_size,)),
             dma((1,)),
-            dma((blocks,)),
             dma((members,)),
             dma((members,)),
             dma((2,)),
@@ -558,6 +611,8 @@
         and seq_size == row_size == 2
         and rest[2].shape[1] == 8 == own * own // LANES
         and seqs * seq_size <= LANES
+        and seqs // 2 % (LANES // 2 // own) == 0
+        and col_size > 2
     )
     path = fast_path if fits else general_path
     return path(alignment_tensor, residue_couplings, first_factor_matrix, *rest)

time: 112 us -> 110 us (0.982)
  Pallas kernels: 97.2 us -> 94.7 us
    pallas_call x1, Pallas kernels: 97.2 us -> 94.7 us  [fast_path(): pl.pallas_call(functools.partial(block_kernel, row_size, col_size, seq_si...]
where the time goes in v3:
time: 110 us; the launch traced here: 109 us
  Pallas kernels  94.7 us (86%)
  local copies, waits for them, and re-layouts  9.82 us (9%)
  other arithmetic  4.12 us (4%)
    pallas_call x1, Pallas kernels, fast_path(): pl.pallas_call(functools.partial(block_kernel, row_size, col_size, seq_si...  94.7 us
    unnamed x4, local copies, waits for them, and re-layouts  9.82 us
    concatenate x2, other arithmetic, twice(): jnp.concatenate([jnp.concatenate([matrix, zero], axis=1), jnp.concatenate...  2.59 us

profile of v3, /device:TPU:0, one launch (start us, length us, event | category | flops | bytes accessed | tf_op | source)
XLA Modules:
  0.0 109.3 jit_solution(966885758042622508)
XLA Ops:
  0.6 1.5 %fusion = (f32[64,128]{1,0:T(8,128)}, f32[64,128]{1,0:T(8,128)}) fusion(f32[64,32]{0,1:T(8,128)} %param.12, f32[64,32]{0,1:T(8,128)} %param.11), kind=kLoop, calls=%fused_computation.8 | loop fusion | flops 65536 | bytes 81920 | tf_op jit(solution)/shard_map/transpose | solution.py:588
  2.2 0.9 copy.12
  3.1 0.8 select_maximum_fusion.final_ref
  3.9 2.0 %copy.11 = f32[1024,128]{0,1:T(8,128)} copy(f32[1024,128]{1,0:T(8,128)} %param.13) | data formatting | bytes 1048576 | tf_op args[4]
  5.9 1.8 %select_maximum_fusion.1 = (f32[128,512]{1,0:T(8,128)}, f32[128,512]{1,0:T(8,128)}) fusion(f32[64,256]{1,0:T(8,128)} %param.16, f32[64,256]{1,0:T(8,128)} %param.15), kind=kLoop, calls=%fused_computation.3 | loop fusion | flops 524288 | bytes 655360 | tf_op jit(solution)/shard_map/concatenate | solution.py:519
  7.7 94.7 %shard_map.104 = (f32[48,32,64]{2,1,0:T(8,128)}, f32[128,64,128]{2,1,0:T(8,128)}) custom-call(f32[48,32,64]{2,1,0:T(8,128)} %bitcast.12, f32[128,64,128]{2,1,0:T(8,128)} %pair_ref.1, f32[64,128]{1,0:T(8,128)} %get-tuple-element.11.first_ref, f32[64,128]{1,0:T(8,128)} %get-tuple-element.10.second_ref, f32[128,1024]{1,0:T(8,128)} %bitcast.10, ...), custom_call_target="tpu_custom_call" | custom-call | tf_op jit(solution)/shard_map/pallas_call | solution.py:549
  102.4 2.1 %copy.17 = f32[48,1,32,64]{3,2,1,0:T(8,128)} copy(f32[48,1,32,64]{3,2,1,0:T(8,128)} %bitcast.11) | data formatting | bytes 786432
  104.5 4.8 %copy.18 = f32[128,64,128]{2,1,0:T(8,128)} copy(f32[128,64,128]{2,1,0:T(8,128)} %get-tuple-element.15) | data formatting | bytes 8388608
